TPU v7x, 32 devices: a whole 2x2x4 slice. The times are simulated.
32 devices in a mesh: rows: 8 (over z, y), cols: 4 (over x, core).
Axes of the slice: x: 2, y: 2, z: 4, core: 2. Of those that a mesh axis runs over, the one named last changes fastest.
Arguments:
- basis_cols: bfloat16 [32768, 1024], P('rows', 'cols'), may hold values from -6 to 6, as said below
- snapshots: bfloat16 [256, 32768], P(None, 'rows'), may hold values from -600 to 600
Outputs:
- coefficients: float32 [1024, 256], P('cols')
- factor: float32 [256, 256], replicated
- directions: bfloat16 [256, 32768], P(None, ('rows', 'cols'))
Inputs may be any that keep to these rules, and one draw needn't show every extreme that they name: `basis_cols`: normal entries.
All inputs are finite; a program needn't handle non-finite values.
Results may differ from a plain program's by a relative error of at most 0.0056.
Values may be sent and summed in bfloat16 or wider, within the bound.
No kernel may reach another device: no remote copies, remote signals or barrier semaphores. Data moves between devices by JAX's collectives and lax.ppermute only.
A program may use at most 64 MiB of HBM per device.

v0:
```python
import functools
import math

import jax
import jax.numpy as jnp
from jax import lax
from jax.experimental import pallas as pl
from jax.experimental.pallas import tpu as pltpu
from jax.sharding import PartitionSpec as P


RANK = 1024
LANES = 128
BLOCK = 32
STEP = 16
SUB = 8


def swap(value, masks):
    count = lax.axis_size("rows") * lax.axis_size("cols")
    return lax.ppermute(value, ("rows", "cols"), [(i, i ^ masks[i % 2]) for i in range(count)])


def bits(count, step=1):
    found = []
    while count > 1:
        found.append(step)
        step, count = 2 * step, count // 2
    return found


def exchange_rounds(masks):
    rounds = [(masks[at], masks[at + 1] if at + 1 < len(masks) else 0) for at in range(0, len(masks), 2)]
    paired = [pair for pair in rounds if pair[1]]
    single = [pair for pair in rounds if not pair[1]]
    return paired + single, paired[::-1] + single


def wide_split(value):
    high = value.astype(jnp.bfloat16)
    return high, (value - high.astype(jnp.float32)).astype(jnp.bfloat16)


def nt_dot(left, right):
    return lax.dot_general(left, right, (((1,), (1,)), ((), ())), preferred_element_type=jnp.float32)


def tn_dot(left, right):
    return lax.dot_general(left, right, (((0,), (0,)), ((), ())), preferred_element_type=jnp.float32)


def slab_copies(whole_ref, into_refs, sem_ref, first, by_rows):
    copies = []
    for index, into_ref in enumerate(into_refs):
        size = into_ref.shape[0 if by_rows else 1]
        start = pl.multiple_of((lax.axis_index("cols") ^ (first + index)) * size, size)
        span = whole_ref.at[pl.ds(start, size), :] if by_rows else whole_ref.at[:, pl.ds(start, size)]
        copies.append(pltpu.make_async_copy(span, into_ref, sem_ref.at[index]))
    return copies


def quad_index(first, second):
    column = lax.axis_index("cols")
    flat = lax.axis_index("rows") * lax.axis_size("cols") + column
    low, high = (flat // jnp.where(column % 2 == 0, *masks) % 2 for masks in (first, second))
    return (low + 2 * high).astype(jnp.int32)


def project_kernel(first, second, basis_ref, snaps_ref, *refs):
    count = (len(refs) - 7) // 2
    piece_refs, slab_refs = refs[:4], (refs[3 + count],) + refs[4 : 3 + count]
    part_refs, total_ref, basis_sem, snaps_sem = refs[4 + count : 4 + 2 * count], refs[-3], refs[-2], refs[-1]
    basis_copies = slab_copies(basis_ref, slab_refs, basis_sem, 0, True)
    snaps_copies = slab_copies(snaps_ref, part_refs, snaps_sem, 0, False)
    for pair in zip(basis_copies, snaps_copies):
        for copy in pair:
            copy.start()
    total = None
    for offset in range(count):
        basis_copies[offset].wait()
        snaps_copies[offset].wait()
        value = jnp.dot(part_refs[offset][...], slab_refs[offset][...], preferred_element_type=jnp.float32)
        total = value if total is None else total + value
    total_ref[...] = total
    rows = piece_refs[0].shape[0]
    quad = quad_index(first, second)
    for offset, piece_ref in enumerate(piece_refs):
        start = pl.multiple_of((quad ^ offset) * rows, rows)
        piece_ref[...] = total_ref[pl.ds(start, rows), :]


def recon_kernel(basis_ref, snaps_ref, low_ref, near_low_ref, near_ref, base_ref, coefficients_ref, *scratch):
    own_ref, span_ref, basis_sem, snaps_sem = scratch
    (basis_copy,) = slab_copies(basis_ref, (own_ref,), basis_sem, 0, True)
    (snaps_copy,) = slab_copies(snaps_ref, (span_ref,), snaps_sem, 0, False)
    basis_copy.start()
    snaps_copy.start()
    coefficients_ref[...] = low_ref[...].astype(jnp.float32).T
    basis_copy.wait()
    snaps_copy.wait()
    chunk = 256
    for start in range(0, base_ref.shape[1], chunk):
        cols = slice(start, start + chunk)
        recon = nt_dot(low_ref[...], own_ref[cols, :]) + nt_dot(near_low_ref[...], near_ref[cols, :])
        base_ref[:, cols] = span_ref[:, cols].astype(jnp.float32) - recon * (1.0 / math.sqrt(RANK))


def packed_rows(tiles):
    return tiles // 2 * (LANES + 2 * SUB) + tiles * (tiles - 1) // 2 * LANES


def pack_layout(tiles):
    at, pairs, blocks = 0, [], []
    for first in range(0, tiles, 2):
        pairs.append((first, at, at + LANES))
        at += LANES + 2 * SUB
    for row in range(tiles):
        for col in range(row + 1, tiles):
            blocks.append((row, col, at))
            at += LANES
    return pairs, blocks


def square_iota(dim):
    return lax.broadcasted_iota(jnp.int32, (LANES, LANES), dim)


def residual_kernel(total_points, *refs):
    count = (len(refs) - 6) // 2
    low_refs, basis_refs = refs[:count], refs[count : 2 * count]
    base_ref, high_ref, rest_ref, keep_ref, send_ref, pack_ref = refs[2 * count :]
    snaps, points = base_ref.shape
    chunk = 256
    for start in range(0, points, chunk):
        cols = slice(start, start + chunk)
        recon = nt_dot(low_refs[0][...], basis_refs[0][cols, :])
        for low_ref, basis_ref in zip(low_refs[1:], basis_refs[1:]):
            recon += nt_dot(low_ref[...], basis_ref[cols, :])
        high, rest = wide_split(base_ref[:, cols] - recon * (1.0 / math.sqrt(RANK)))
        high_ref[:, cols] = high
        rest_ref[:, cols] = rest
    scale = 1.0 / total_points

    high, rest = high_ref[...], rest_ref[...]
    gram = (nt_dot(high, high) + (nt_dot(high, rest) + nt_dot(rest, high))) * scale

    def block(row, col):
        return gram[row * LANES : (row + 1) * LANES, col * LANES : (col + 1) * LANES]

    pairs, blocks = pack_layout(snaps // LANES)
    down, across = square_iota(0), square_iota(1)
    for first, at, line in pairs:
        upper, lower = block(first, first), block(first + 1, first + 1)
        pack_ref[pl.ds(at, LANES), :] = jnp.where(down <= across, upper, lower)
        diagonal = jnp.sum(jnp.where(down == across, lower, 0.0), axis=0, keepdims=True)
        pack_ref[pl.ds(line, 2 * SUB), :] = jnp.broadcast_to(diagonal, (2 * SUB, LANES))
    for row, col, at in blocks:
        pack_ref[pl.ds(at, LANES), :] = block(row, col)
    half = pack_ref.shape[0] // 2
    odd = lax.axis_index("cols") % 2 == 1
    first, second = pack_ref[pl.ds(0, half), :], pack_ref[pl.ds(half, half), :]
    keep_ref[...] = jnp.where(odd, second, first)
    send_ref[...] = jnp.where(odd, first, second)


def row_of(tile, index):
    return jnp.broadcast_to(tile[index : index + 1, :], tile.shape)


def eliminate(panel, offset):
    groups = BLOCK // SUB
    sub_iota = lax.broadcasted_iota(jnp.int32, (SUB, LANES), 0)
    scales = [jnp.zeros((SUB, LANES), jnp.float32) for _ in range(groups)]
    for begin in range(0, BLOCK, STEP):
        columns = [
            [
                jnp.broadcast_to(panel[0][g][:, offset + j : offset + j + 1], (SUB, LANES))
                if g >= begin // SUB
                else None
                for g in range(groups)
            ]
            for j in range(begin, begin + STEP)
        ]
        for p in range(begin, begin + STEP, 2):
            home, line = divmod(p, SUB)
            left, right = columns[p - begin], columns[p + 1 - begin]
            pivot, cross = row_of(left[home], line), row_of(left[home], line + 1)
            both = pivot * row_of(right[home], line + 1) - cross * cross
            inverse = 1.0 / pivot
            second = pivot * (1.0 / both)
            ratio = cross * inverse
            scales[home] = jnp.where(sub_iota == line, lax.rsqrt(pivot), scales[home])
            scales[home] = jnp.where(sub_iota == line + 1, lax.rsqrt(both * inverse), scales[home])
            right = [None if tile is None else tile - ratio * left[g] for g, tile in enumerate(right)]
            below, under = list(left), list(right)
            below[home] = jnp.where(sub_iota > line, left[home], 0.0)
            under[home] = jnp.where(sub_iota > line + 1, right[home], 0.0)
            last = home + 1 if line + 2 == SUB else home
            for j in range(p + 2, begin + STEP):
                lanes, first = columns[j - begin], j // SUB
                lead, next_lead = row_of(left[first], j % SUB) * inverse, row_of(right[first], j % SUB) * second
                for g in range(max(first, last), groups):
                    lanes[g] = (lanes[g] - below[g] * lead) - under[g] * next_lead
            for lanes in panel:
                top = row_of(lanes[home], line)
                lead, next_lead = top * inverse, (row_of(lanes[home], line + 1) - ratio * top) * second
                for g in range(home, groups):
                    lanes[g] = lanes[g] - below[g] * lead
                    if g >= last:
                        lanes[g] = lanes[g] - under[g] * next_lead
    return [[tile * scale for tile, scale in zip(lanes, scales)] for lanes in panel]


def factor_kernel(mine_ref, other_ref, high_ref, rest_ref, factor_out_ref, directions_ref, *scratch):
    factor_ref, out_ref, a_ref, w_ref, pack_ref, factor_sem, out_sem = scratch
    size = factor_ref.shape[0]
    tiles = size // LANES
    half = mine_ref.shape[0]
    odd = lax.axis_index("cols") % 2 == 1
    pack_ref[pl.ds(0, half), :] = jnp.where(odd, other_ref[...], mine_ref[...])
    pack_ref[pl.ds(half, half), :] = jnp.where(odd, mine_ref[...], other_ref[...])
    pairs, blocks = pack_layout(tiles)
    down, across = square_iota(0), square_iota(1)

    def square(tile):
        return pl.ds(tile * LANES, LANES), pl.ds(tile * LANES, LANES)

    diagonals = {}
    for first, at, line in pairs:
        inner = jnp.where(down == across, pack_ref[pl.ds(at, LANES), :], 0.0)
        diagonals[first] = jnp.sum(inner, axis=0, keepdims=True)
        diagonals[first + 1] = pack_ref[pl.ds(line, 1), :]
    rows_by = [jnp.broadcast_to(lax.rsqrt(diagonals[tile]), (LANES, LANES)) for tile in range(tiles)]
    roots = [diagonals[tile] * lax.rsqrt(diagonals[tile]) for tile in range(tiles)]
    down_by = [value.T for value in rows_by]

    for first, at, line in pairs:
        folded = pack_ref[pl.ds(at, LANES), :]
        turned = folded.T
        value = jnp.where(down <= across, folded, turned)
        a_ref[square(first)] = value * down_by[first] * rows_by[first]
        diagonal = jnp.broadcast_to(diagonals[first + 1], (LANES, LANES))
        value = jnp.where(down == across, diagonal, jnp.where(down > across, folded, turned))
        a_ref[square(first + 1)] = value * down_by[first + 1] * rows_by[first + 1]
    for row, col, at in blocks:
        value = pack_ref[pl.ds(at, LANES), :] * down_by[row] * rows_by[col]
        a_ref[pl.ds(row * LANES, LANES), pl.ds(col * LANES, LANES)] = value
    w_ref[...] = jnp.zeros((size, size), jnp.float32)
    for tile in range(tiles):
        w_ref[square(tile)] = jnp.where(down == across, rows_by[tile], 0.0)

    def row_copies(row):
        rows = pl.ds(row * LANES, LANES)
        return (
            pltpu.make_async_copy(factor_ref.at[rows, :], factor_out_ref.at[rows, :], factor_sem.at[row]),
            pltpu.make_async_copy(out_ref.at[rows, :], directions_ref.at[rows, :], out_sem.at[row]),
        )

    def update_rest(places, panel, a_tiles, after):
        parts = [wide_split(value) for value in panel]
        left = [jnp.concatenate([a, a, b], axis=0) for a, b in parts[: len(a_tiles)]]
        right = [jnp.concatenate([a, b, a], axis=0) for a, b in parts]
        for row_tile in a_tiles:
            skip = max(after - row_tile * LANES, 0)
            if skip == LANES:
                continue
            rows = pl.ds(row_tile * LANES + skip, LANES - skip)
            used = [(place, value) for place, value in zip(places, right) if place[0] is w_ref or place[1] >= row_tile]
            wide = tn_dot(left[row_tile - a_tiles[0]], jnp.concatenate([value for _, value in used], axis=1))
            for index, ((ref, t), _) in enumerate(used):
                lanes = pl.ds(t * LANES, LANES)
                ref[rows, lanes] = ref[rows, lanes] - wide[skip:, index * LANES : (index + 1) * LANES]

    def emit(row):
        rows = pl.ds(row * LANES, LANES)
        for col in range(tiles):
            into = (rows, pl.ds(col * LANES, LANES))
            if row < col:
                factor_ref[into] = jnp.zeros((LANES, LANES), jnp.float32)
                continue
            block = (a_ref[pl.ds(col * LANES, LANES), rows] * roots[row]).T
            factor_ref[into] = jnp.where(down >= across, block, 0.0) if row == col else block
        depth, chunk = (row + 1) * LANES, 256
        high, rest = wide_split(w_ref[rows, pl.ds(0, depth)])
        for start in range(0, out_ref.shape[1], chunk):
            cols = pl.ds(start, chunk)
            right_high, right_rest = high_ref[pl.ds(0, depth), cols], rest_ref[pl.ds(0, depth), cols]
            value = jnp.dot(high, right_high, preferred_element_type=jnp.float32)
            value += jnp.dot(high, right_rest, preferred_element_type=jnp.float32)
            value += jnp.dot(rest, right_high, preferred_element_type=jnp.float32)
            out_ref[rows, cols] = value.astype(jnp.bfloat16)

    done_tiles, started = [], 0
    for base in range(0, size, BLOCK):
        tile, offset = divmod(base, LANES)
        a_tiles, w_tiles = range(tile, tiles), range(tile + 1)
        places = [(a_ref, t) for t in a_tiles] + [(w_ref, t) for t in w_tiles]
        panel = [
            [ref[pl.ds(base + g, SUB), pl.ds(t * LANES, LANES)] for g in range(0, BLOCK, SUB)] for ref, t in places
        ]
        panel = [jnp.concatenate(lanes, axis=0) for lanes in eliminate(panel, offset)]
        for (ref, t), value in zip(places, panel):
            ref[pl.ds(base, BLOCK), pl.ds(t * LANES, LANES)] = value
        after = base + BLOCK
        update_rest(places, panel, a_tiles, after)
        if started < len(done_tiles):
            for copy in row_copies(done_tiles[started]):
                copy.start()
            started += 1
        if after % LANES == 0:
            emit(tile)
            done_tiles.append(tile)
    for row in done_tiles[started:]:
        for copy in row_copies(row):
            copy.start()
    for row in done_tiles:
        for copy in row_copies(row):
            copy.wait()


def call(kernel, outs, scratch, flops, grant, whole=0, stay=False):
    vmem = pl.BlockSpec(memory_space=pltpu.VMEM)
    hbm = pl.BlockSpec(memory_space=pltpu.HBM)

    def run(*args):
        size = sum(math.prod(x.shape) * x.dtype.itemsize for x in (*args, *outs))
        args = [pltpu.with_memory_space_constraint(x, pltpu.HBM) for x in args[:whole]] + list(args[whole:])
        return pl.pallas_call(
            kernel,
            out_shape=outs,
            in_specs=[hbm] * whole + [vmem] * (len(args) - whole),
            out_specs=[hbm if stay else vmem] * len(outs),
            scratch_shapes=scratch,
            compiler_params=pltpu.CompilerParams(vmem_limit_bytes=grant << 20),
            cost_estimate=pl.CostEstimate(flops=flops, bytes_accessed=size, transcendentals=0),
        )(*args)

    return run


def shape(dtype, *dims):
    return jax.ShapeDtypeStruct(dims, dtype)


def compute(basis_cols, snapshots):
    snaps, row_points = snapshots.shape
    modes = basis_cols.shape[1]
    row_count, columns = lax.axis_size("rows"), lax.axis_size("cols")
    total_points = row_points * row_count
    points = row_points // columns
    quarter = snaps // 4
    bf16, f32 = jnp.bfloat16, jnp.float32

    row_bits = bits(row_count, columns)
    orders = list(zip(row_bits, row_bits[1:] + row_bits[:1]))
    first, second = orders[0], orders[1]
    both = tuple(a ^ b for a, b in zip(first, second))
    quad = quad_index(first, second)

    slab, piece = shape(bf16, points, modes), shape(f32, quarter, modes)
    slab_scratch, span_scratch = pltpu.VMEM((points, modes), bf16), pltpu.VMEM((snaps, points), bf16)
    semaphores = pltpu.SemaphoreType.DMA((columns,))
    kept, one, two, three, *slabs = call(
        functools.partial(project_kernel, first, second),
        (piece,) * 4 + (slab,) * (columns - 1),
        [slab_scratch] + [span_scratch] * columns + [pltpu.VMEM((snaps, modes), f32), semaphores, semaphores],
        2 * snaps * row_points * modes,
        12,
        2,
    )(basis_cols, snapshots)
    arrived_slabs = [swap(slabs[offset - 1], (offset,) * 2) for offset in range(2, columns)]
    one, two, three = swap(one, first), swap(two, second), swap(three, both)
    near_slab = swap(slabs[0], (1, 1))
    kept = (kept + one) + (two + three)
    for step in orders[2:]:
        kept = kept + swap(kept, step)
    low = (kept * (math.sqrt(RANK) / total_points)).astype(bf16)
    found = (low, swap(low, first), swap(low, second), swap(low, both))
    low = jnp.concatenate([lax.select_n(quad ^ at, *found) for at in range(4)], 0)
    lows = {0: low}
    for offset in range(2, columns, 2):
        lows[offset] = swap(low, (offset, offset))
    for offset in range(0, columns, 2):
        lows[offset + 1] = swap(lows[offset], (1, 1))

    begun, coefficients = call(
        recon_kernel,
        (shape(f32, snaps, points), shape(f32, modes, snaps)),
        [slab_scratch, span_scratch, semaphores, semaphores],
        4 * snaps * points * modes,
        8,
        2,
    )(basis_cols, snapshots, lows[0], lows[1], near_slab)
    packed = packed_rows(snaps // LANES)
    part = shape(f32, packed // 2, LANES)
    wide = shape(bf16, snaps, points)
    high, rest, keep, send = call(
        functools.partial(residual_kernel, total_points),
        (wide, wide, part, part),
        [pltpu.VMEM((packed, LANES), f32)],
        2 * snaps * points * (modes * (columns - 2) + 3 * snaps),
        16,
    )(*[lows[offset] for offset in range(2, columns)], *arrived_slabs, begun)
    keep = keep + swap(send, (1, 1))
    for masks in zip(*exchange_rounds(bits(columns // 2, 2) + row_bits)):
        if masks[0][1] == 0:
            keep = keep + swap(keep, [mask[0] for mask in masks])
            continue
        far = swap(keep, [mask[1] for mask in masks])
        diagonal = swap(keep, [mask[0] ^ mask[1] for mask in masks])
        keep = (keep + swap(keep, [mask[0] for mask in masks])) + (far + diagonal)
    rest_of_gram = swap(keep, (1, 1))
    factor, directions = call(
        factor_kernel,
        (shape(f32, snaps, snaps), wide),
        [pltpu.VMEM((snaps, snaps), f32), span_scratch]
        + [pltpu.VMEM((snaps, snaps), f32)] * 2
        + [pltpu.VMEM((packed, LANES), f32)]
        + [pltpu.SemaphoreType.DMA((snaps // LANES,))] * 2,
        6 * snaps * snaps * points,
        16,
        stay=True,
    )(keep, rest_of_gram, high, rest)
    return (coefficients, factor, directions)


def solution(mesh):
    placed = (P("rows", "cols"), P(None, "rows"))
    return jax.shard_map(
        compute,
        mesh=mesh,
        in_specs=placed,
        out_specs=(P("cols", None), P(), P(None, ("rows", "cols"))),
        check_vma=False,
    )
```

profile of v0, /device:TPU:0, one launch (start us, length us, event | category | flops | bytes accessed | tf_op | source)
XLA Modules:
  0.0 80.7 jit_solution(13981620555559035303)
XLA Ops:
  0.6 3.0 %shard_map.49 = (f32[64,256]{1,0:T(8,128)S(1)}, f32[64,256]{1,0:T(8,128)S(1)}, f32[64,256]{1,0:T(8,128)S(1)}, f32[64,256]{1,0:T(8,128)S(1)}, bf16[1024,256]{1,0:...) custom-call(bf16[4096,256]{1,0:T(8,128)(2,1)} %basis_ref.3, bf16[256,4096]{1,0:T(8,128)(2,1)} %snaps_ref.3), custom_call_target="tpu_custom_call" | custom-call | flops 536870912 | bytes 6029312 | tf_op jit(solution)/shard_map/pallas_call | solution.py:328
  3.7 3.1 %collective-permute-start = (f32[64,256]{1,0:T(8,128)S(1)}, f32[64,256]{1,0:T(8,128)S(1)}, u32[]{:S(2)}, u32[]{:S(2)}) collective-permute-start(f32[64,256]{1,0:T(8,128)S(1)} %get-tuple-element.19), channel_id=1, source_target_pairs={{0,4},{1,9},{2,6},{3,11},{4,0},{5,13},{6,2},{7,15},{8,12},{9,1},{1... | collective-permute-start | bytes 196616 | tf_op jit(solution)/shard_map/ppermute | solution.py:21
  6.7 1.6 %collective-permute-start.1 = (f32[64,256]{1,0:T(8,128)S(1)}, f32[64,256]{1,0:T(8,128)S(1)}, u32[]{:S(2)}, u32[]{:S(2)}) collective-permute-start(f32[64,256]{1,0:T(8,128)S(1)} %get-tuple-element.20), channel_id=1, source_target_pairs={{0,8},{1,17},{2,10},{3,19},{4,12},{5,21},{6,14},{7,23},{8,0},{9,25... | collective-permute-start | bytes 196616 | tf_op jit(solution)/shard_map/ppermute | solution.py:21
  8.3 0.7 collective-permute-done
  9.0 2.2 %collective-permute-done.1 = f32[64,256]{1,0:T(8,128)S(1)} collective-permute-done((f32[64,256]{1,0:T(8,128)S(1)}, f32[64,256]{1,0:T(8,128)S(1)}, u32[]{:S(2)}, u32[]{:S(2)}) %collective-permute-start.1) | collective-permute-done | bytes 65568 | tf_op jit(solution)/shard_map/ppermute | solution.py:21
  11.2 2.3 %collective-permute-done.2 = f32[64,256]{1,0:T(8,128)S(1)} collective-permute-done((f32[64,256]{1,0:T(8,128)S(1)}, f32[64,256]{1,0:T(8,128)S(1)}, u32[]{:S(2)}, u32[]{:S(2)}) %collective-permute-start.2) | collective-permute-done | bytes 65568 | tf_op jit(solution)/shard_map/ppermute | solution.py:21
  13.5 2.7 %collective-permute-start.3 = (f32[64,256]{1,0:T(8,128)S(1)}, f32[64,256]{1,0:T(8,128)S(1)}, u32[]{:S(2)}, u32[]{:S(2)}) collective-permute-start(f32[64,256]{1,0:T(8,128)S(1)} %add_add_fusion.2), channel_id=1, source_target_pairs={{0,16},{1,5},{2,18},{3,7},{4,20},{5,1},{6,22},{7,3},{8,24},{9,13},... | collective-permute-start | bytes 196616 | tf_op jit(solution)/shard_map/ppermute | solution.py:21
  16.1 3.5 %collective-permute-done.3 = f32[64,256]{1,0:T(8,128)S(1)} collective-permute-done((f32[64,256]{1,0:T(8,128)S(1)}, f32[64,256]{1,0:T(8,128)S(1)}, u32[]{:S(2)}, u32[]{:S(2)}) %collective-permute-start.3) | collective-permute-done | bytes 65568 | tf_op jit(solution)/shard_map/ppermute | solution.py:21
  19.7 0.9 %collective-permute-start.6 = (bf16[64,256]{1,0:T(8,128)(2,1)S(1)}, bf16[64,256]{1,0:T(8,128)(2,1)S(1)}, u32[]{:S(2)}, u32[]{:S(2)}) collective-permute-start(bf16[64,256]{1,0:T(8,128)(2,1)S(1)} %multiply_convert_fusion), channel_id=1, source_target_pairs={{0,12},{1,25},{2,14},{3,27},{4,8},{5,29},{6,10},{7,31},{8,4},{9,17... | collective-permute-start | bytes 98312 | tf_op jit(solution)/shard_map/ppermute | solution.py:21
  20.6 0.2 collective-permute-start.5
  20.8 2.5 %collective-permute-start.4 = (bf16[64,256]{1,0:T(8,128)(2,1)S(1)}, bf16[64,256]{1,0:T(8,128)(2,1)S(1)}, u32[]{:S(2)}, u32[]{:S(2)}) collective-permute-start(bf16[64,256]{1,0:T(8,128)(2,1)S(1)} %multiply_convert_fusion), channel_id=1, source_target_pairs={{0,4},{1,9},{2,6},{3,11},{4,0},{5,13},{6,2},{7,15},{8,12},{9,1},{1... | collective-permute-start | bytes 98312 | tf_op jit(solution)/shard_map/ppermute | solution.py:21
  23.3 1.5 %collective-permute-start.11 = (bf16[1024,256]{1,0:T(8,128)(2,1)S(1)}, bf16[1024,256]{1,0:T(8,128)(2,1)S(1)}, u32[]{:S(2)}, u32[]{:S(2)}) collective-permute-start(bf16[1024,256]{1,0:T(8,128)(2,1)S(1)} %get-tuple-element.24), channel_id=1, source_target_pairs={{0,2},{1,3},{2,0},{3,1},{4,6},{5,7},{6,4},{7,5},{8,10},{9,11},{10,... | collective-permute-start | bytes 1572872 | tf_op jit(solution)/shard_map/ppermute | solution.py:21
  24.8 0.4 collective-permute-start.12
  25.2 1.6 %collective-permute-start.9 = (bf16[256,256]{1,0:T(8,128)(2,1)S(1)}, bf16[256,256]{1,0:T(8,128)(2,1)S(1)}, u32[]{:S(2)}, u32[]{:S(2)}) collective-permute-start(bf16[256,256]{1,0:T(8,128)(2,1)S(1)} %pad_maximum_fusion.low_ref), channel_id=1, source_target_pairs={{0,2},{1,3},{2,0},{3,1},{4,6},{5,7},{6,4},{7,5},{8,10},{9,11},{10,... | collective-permute-start | bytes 393224 | tf_op jit(solution)/shard_map/ppermute | solution.py:21
  26.8 24.9 %collective-permute-done.9.refs_0_ = bf16[256,256]{1,0:T(8,128)(2,1)S(1)} collective-permute-done((bf16[256,256]{1,0:T(8,128)(2,1)S(1)}, bf16[256,256]{1,0:T(8,128)(2,1)S(1)}, u32[]{:S(2)}, u32[]{:S(2)}) %collective-permute-start.9) | collective-permute-done | bytes 131104 | tf_op jit(solution)/shard_map/ppermute | solution.py:21
  51.7 2.3 %shard_map.50 = (f32[256,1024]{1,0:T(8,128)S(1)}, f32[256,256]{1,0:T(8,128)}) custom-call(bf16[4096,256]{1,0:T(8,128)(2,1)} %basis_ref.3, bf16[256,4096]{1,0:T(8,128)(2,1)} %snaps_ref.3, bf16[256,256]{1,0:T(8,128)(2,1)S(1)} %pad_maximum_fusion.low_ref, bf16[256,256]{1,0:T(8,128)(2,1)S(1)} %collective-permute-done.7.near_low_ref, ...), custom_call_target="tpu_custom_call" | custom-call | flops 268435456 | bytes 6291456 | tf_op jit(solution)/shard_map/pallas_call | solution.py:328
  54.0 1.5 %shard_map.51 = (bf16[256,1024]{1,0:T(8,128)(2,1)S(1)}, bf16[256,1024]{1,0:T(8,128)(2,1)S(1)}, f32[136,128]{1,0:T(8,128)S(1)}, f32[136,128]{1,0:T(8,128)S(1)}) custom-call(bf16[256,256]{1,0:T(8,128)(2,1)S(1)} %collective-permute-done.9.refs_0_, bf16[256,256]{1,0:T(8,128)(2,1)S(1)} %collective-permute-done.10.refs_1_, ...), custom_call_target="tpu_custom_call" | custom-call | flops 671088640 | bytes 3547136 | tf_op jit(solution)/shard_map/pallas_call | solution.py:328
  55.5 0.6 collective-permute-start.13
  56.1 0.9 %collective-permute-done.13 = f32[136,128]{1,0:T(8,128)S(1)} collective-permute-done((f32[136,128]{1,0:T(8,128)S(1)}, f32[136,128]{1,0:T(8,128)S(1)}, u32[]{:S(2)}, u32[]{:S(2)}) %collective-permute-start.13) | collective-permute-done | bytes 69664 | tf_op jit(solution)/shard_map/ppermute | solution.py:21
  57.0 1.0 %collective-permute-start.16 = (f32[136,128]{1,0:T(8,128)S(1)}, f32[136,128]{1,0:T(8,128)S(1)}, u32[]{:S(2)}, u32[]{:S(2)}) collective-permute-start(f32[136,128]{1,0:T(8,128)S(1)} %add.61), channel_id=1, source_target_pairs={{0,6},{1,25},{2,4},{3,27},{4,2},{5,29},{6,0},{7,31},{8,14},{9,17},... | collective-permute-start | bytes 208904 | tf_op jit(solution)/shard_map/ppermute | solution.py:21
  58.0 2.0 %collective-permute-start.15 = (f32[136,128]{1,0:T(8,128)S(1)}, f32[136,128]{1,0:T(8,128)S(1)}, u32[]{:S(2)}, u32[]{:S(2)}) collective-permute-start(f32[136,128]{1,0:T(8,128)S(1)} %add.61), channel_id=1, source_target_pairs={{0,4},{1,17},{2,6},{3,19},{4,0},{5,21},{6,2},{7,23},{8,12},{9,25},... | collective-permute-start | bytes 208904 | tf_op jit(solution)/shard_map/ppermute | solution.py:21
  60.0 0.5 collective-permute-start.14
  60.5 1.8 %collective-permute-done.16 = f32[136,128]{1,0:T(8,128)S(1)} collective-permute-done((f32[136,128]{1,0:T(8,128)S(1)}, f32[136,128]{1,0:T(8,128)S(1)}, u32[]{:S(2)}, u32[]{:S(2)}) %collective-permute-start.16) | collective-permute-done | bytes 69664 | tf_op jit(solution)/shard_map/ppermute | solution.py:21
  62.3 0.7 collective-permute-done.15
  63.0 1.3 %collective-permute-done.14 = f32[136,128]{1,0:T(8,128)S(1)} collective-permute-done((f32[136,128]{1,0:T(8,128)S(1)}, f32[136,128]{1,0:T(8,128)S(1)}, u32[]{:S(2)}, u32[]{:S(2)}) %collective-permute-start.14) | collective-permute-done | bytes 69664 | tf_op jit(solution)/shard_map/ppermute | solution.py:21
  64.3 2.9 %collective-permute-start.19 = (f32[136,128]{1,0:T(8,128)S(1)}, f32[136,128]{1,0:T(8,128)S(1)}, u32[]{:S(2)}, u32[]{:S(2)}) collective-permute-start(f32[136,128]{1,0:T(8,128)S(1)} %add_add_fusion.1), channel_id=1, source_target_pairs={{0,24},{1,7},{2,26},{3,5},{4,28},{5,3},{6,30},{7,1},{8,16},{9,15},... | collective-permute-start | bytes 208904 | tf_op jit(solution)/shard_map/ppermute | solution.py:21
  67.2 1.6 %collective-permute-start.17 = (f32[136,128]{1,0:T(8,128)S(1)}, f32[136,128]{1,0:T(8,128)S(1)}, u32[]{:S(2)}, u32[]{:S(2)}) collective-permute-start(f32[136,128]{1,0:T(8,128)S(1)} %add_add_fusion.1), channel_id=1, source_target_pairs={{0,8},{1,3},{2,10},{3,1},{4,12},{5,7},{6,14},{7,5},{8,0},{9,11},{1... | collective-permute-start | bytes 208904 | tf_op jit(solution)/shard_map/ppermute | solution.py:21
  68.8 1.7 %collective-permute-done.19 = f32[136,128]{1,0:T(8,128)S(1)} collective-permute-done((f32[136,128]{1,0:T(8,128)S(1)}, f32[136,128]{1,0:T(8,128)S(1)}, u32[]{:S(2)}, u32[]{:S(2)}) %collective-permute-start.19) | collective-permute-done | bytes 69664 | tf_op jit(solution)/shard_map/ppermute | solution.py:21
  70.5 1.9 %collective-permute-done.18 = f32[136,128]{1,0:T(8,128)S(1)} collective-permute-done((f32[136,128]{1,0:T(8,128)S(1)}, f32[136,128]{1,0:T(8,128)S(1)}, u32[]{:S(2)}, u32[]{:S(2)}) %collective-permute-start.18) | collective-permute-done | bytes 69664 | tf_op jit(solution)/shard_map/ppermute | solution.py:21
  72.4 0.1 collective-permute-start.20
  72.5 1.2 %collective-permute-done.20.other_ref = f32[136,128]{1,0:T(8,128)S(1)} collective-permute-done((f32[136,128]{1,0:T(8,128)S(1)}, f32[136,128]{1,0:T(8,128)S(1)}, u32[]{:S(2)}, u32[]{:S(2)}) %collective-permute-start.20) | collective-permute-done | bytes 69664 | tf_op jit(solution)/shard_map/ppermute | solution.py:21
  73.7 7.0 %shard_map.52 = (f32[256,256]{1,0:T(8,128)}, bf16[256,1024]{1,0:T(8,128)(2,1)}) custom-call(f32[136,128]{1,0:T(8,128)S(1)} %add_add_fusion.mine_ref, f32[136,128]{1,0:T(8,128)S(1)} %collective-permute-done.20.other_ref, bf16[256,1024]{1,0:T(8,128)(2,1)S(1)} %get-tuple-element.29.high_ref, bf16[256,1024]{1,0:T(8,128)(2,1)S(1)} %get-tuple-element.30.rest_ref), custom_call_target="tpu_custom_call" | custom-call | flops 402653184 | bytes 1974272 | tf_op jit(solution)/shard_map/pallas_call | solution.py:328
  (21 shorter events, 0.2 us)
Async XLA Ops:
  3.7 5.3 %collective-permute-start = (f32[64,256]{1,0:T(8,128)S(1)}, f32[64,256]{1,0:T(8,128)S(1)}, u32[]{:S(2)}, u32[]{:S(2)}) collective-permute-start(f32[64,256]{1,0:T(8,128)S(1)} %get-tuple-element.19), channel_id=1, source_target_pairs={{0,4},{1,9},{2,6},{3,11},{4,0},{5,13},{6,2},{7,15},{8,12},{9,1},{1... | collective-permute-start | bytes 196616 | tf_op jit(solution)/shard_map/ppermute | solution.py:21
  6.7 4.4 %collective-permute-start.1 = (f32[64,256]{1,0:T(8,128)S(1)}, f32[64,256]{1,0:T(8,128)S(1)}, u32[]{:S(2)}, u32[]{:S(2)}) collective-permute-start(f32[64,256]{1,0:T(8,128)S(1)} %get-tuple-element.20), channel_id=1, source_target_pairs={{0,8},{1,17},{2,10},{3,19},{4,12},{5,21},{6,14},{7,23},{8,0},{9,25... | collective-permute-start | bytes 196616 | tf_op jit(solution)/shard_map/ppermute | solution.py:21
  8.3 5.2 %collective-permute-start.2 = (f32[64,256]{1,0:T(8,128)S(1)}, f32[64,256]{1,0:T(8,128)S(1)}, u32[]{:S(2)}, u32[]{:S(2)}) collective-permute-start(f32[64,256]{1,0:T(8,128)S(1)} %get-tuple-element.21), channel_id=1, source_target_pairs={{0,12},{1,25},{2,14},{3,27},{4,8},{5,29},{6,10},{7,31},{8,4},{9,17... | collective-permute-start | bytes 196616 | tf_op jit(solution)/shard_map/ppermute | solution.py:21
  13.5 6.2 %collective-permute-start.3 = (f32[64,256]{1,0:T(8,128)S(1)}, f32[64,256]{1,0:T(8,128)S(1)}, u32[]{:S(2)}, u32[]{:S(2)}) collective-permute-start(f32[64,256]{1,0:T(8,128)S(1)} %add_add_fusion.2), channel_id=1, source_target_pairs={{0,16},{1,5},{2,18},{3,7},{4,20},{5,1},{6,22},{7,3},{8,24},{9,13},... | collective-permute-start | bytes 196616 | tf_op jit(solution)/shard_map/ppermute | solution.py:21
  19.7 5.1 %collective-permute-start.6 = (bf16[64,256]{1,0:T(8,128)(2,1)S(1)}, bf16[64,256]{1,0:T(8,128)(2,1)S(1)}, u32[]{:S(2)}, u32[]{:S(2)}) collective-permute-start(bf16[64,256]{1,0:T(8,128)(2,1)S(1)} %multiply_convert_fusion), channel_id=1, source_target_pairs={{0,12},{1,25},{2,14},{3,27},{4,8},{5,29},{6,10},{7,31},{8,4},{9,17... | collective-permute-start | bytes 98312 | tf_op jit(solution)/shard_map/ppermute | solution.py:21
  20.6 4.6 %collective-permute-start.5 = (bf16[64,256]{1,0:T(8,128)(2,1)S(1)}, bf16[64,256]{1,0:T(8,128)(2,1)S(1)}, u32[]{:S(2)}, u32[]{:S(2)}) collective-permute-start(bf16[64,256]{1,0:T(8,128)(2,1)S(1)} %multiply_convert_fusion), channel_id=1, source_target_pairs={{0,8},{1,17},{2,10},{3,19},{4,12},{5,21},{6,14},{7,23},{8,0},{9,25... | collective-permute-start | bytes 98312 | tf_op jit(solution)/shard_map/ppermute | solution.py:21
  20.8 4.4 %collective-permute-start.4 = (bf16[64,256]{1,0:T(8,128)(2,1)S(1)}, bf16[64,256]{1,0:T(8,128)(2,1)S(1)}, u32[]{:S(2)}, u32[]{:S(2)}) collective-permute-start(bf16[64,256]{1,0:T(8,128)(2,1)S(1)} %multiply_convert_fusion), channel_id=1, source_target_pairs={{0,4},{1,9},{2,6},{3,11},{4,0},{5,13},{6,2},{7,15},{8,12},{9,1},{1... | collective-permute-start | bytes 98312 | tf_op jit(solution)/shard_map/ppermute | solution.py:21
  23.3 28.4 %collective-permute-start.8 = (bf16[1024,256]{1,0:T(8,128)(2,1)S(1)}, bf16[1024,256]{1,0:T(8,128)(2,1)S(1)}, u32[]{:S(2)}, u32[]{:S(2)}) collective-permute-start(bf16[1024,256]{1,0:T(8,128)(2,1)S(1)} %get-tuple-element.22), channel_id=1, source_target_pairs={{0,1},{1,0},{2,3},{3,2},{4,5},{5,4},{6,7},{7,6},{8,9},{9,8},{10,11... | collective-permute-start | bytes 1572872 | tf_op jit(solution)/shard_map/ppermute | solution.py:21
  23.3 30.7 %collective-permute-start.11 = (bf16[1024,256]{1,0:T(8,128)(2,1)S(1)}, bf16[1024,256]{1,0:T(8,128)(2,1)S(1)}, u32[]{:S(2)}, u32[]{:S(2)}) collective-permute-start(bf16[1024,256]{1,0:T(8,128)(2,1)S(1)} %get-tuple-element.24), channel_id=1, source_target_pairs={{0,2},{1,3},{2,0},{3,1},{4,6},{5,7},{6,4},{7,5},{8,10},{9,11},{10,... | collective-permute-start | bytes 1572872 | tf_op jit(solution)/shard_map/ppermute | solution.py:21
  24.8 29.2 %collective-permute-start.12 = (bf16[1024,256]{1,0:T(8,128)(2,1)S(1)}, bf16[1024,256]{1,0:T(8,128)(2,1)S(1)}, u32[]{:S(2)}, u32[]{:S(2)}) collective-permute-start(bf16[1024,256]{1,0:T(8,128)(2,1)S(1)} %get-tuple-element.25), channel_id=1, source_target_pairs={{0,3},{1,2},{2,1},{3,0},{4,7},{5,6},{6,5},{7,4},{8,11},{9,10},{10,... | collective-permute-start | bytes 1572872 | tf_op jit(solution)/shard_map/ppermute | solution.py:21
  25.2 26.4 %collective-permute-start.9 = (bf16[256,256]{1,0:T(8,128)(2,1)S(1)}, bf16[256,256]{1,0:T(8,128)(2,1)S(1)}, u32[]{:S(2)}, u32[]{:S(2)}) collective-permute-start(bf16[256,256]{1,0:T(8,128)(2,1)S(1)} %pad_maximum_fusion.low_ref), channel_id=1, source_target_pairs={{0,2},{1,3},{2,0},{3,1},{4,6},{5,7},{6,4},{7,5},{8,10},{9,11},{10,... | collective-permute-start | bytes 393224 | tf_op jit(solution)/shard_map/ppermute | solution.py:21
  26.7 24.9 %collective-permute-start.7 = (bf16[256,256]{1,0:T(8,128)(2,1)S(1)}, bf16[256,256]{1,0:T(8,128)(2,1)S(1)}, u32[]{:S(2)}, u32[]{:S(2)}) collective-permute-start(bf16[256,256]{1,0:T(8,128)(2,1)S(1)} %pad_maximum_fusion.low_ref), channel_id=1, source_target_pairs={{0,1},{1,0},{2,3},{3,2},{4,5},{5,4},{6,7},{7,6},{8,9},{9,8},{10,11... | collective-permute-start | bytes 393224 | tf_op jit(solution)/shard_map/ppermute | solution.py:21
  51.6 2.3 %collective-permute-start.10 = (bf16[256,256]{1,0:T(8,128)(2,1)S(1)}, bf16[256,256]{1,0:T(8,128)(2,1)S(1)}, u32[]{:S(2)}, u32[]{:S(2)}) collective-permute-start(bf16[256,256]{1,0:T(8,128)(2,1)S(1)} %collective-permute-done.9.refs_0_), channel_id=1, source_target_pairs={{0,1},{1,0},{2,3},{3,2},{4,5},{5,4},{6,7},{7,6},{8,9},{9,8},{10,11... | collective-permute-start | bytes 393224 | tf_op jit(solution)/shard_map/ppermute | solution.py:21
  55.5 1.5 %collective-permute-start.13 = (f32[136,128]{1,0:T(8,128)S(1)}, f32[136,128]{1,0:T(8,128)S(1)}, u32[]{:S(2)}, u32[]{:S(2)}) collective-permute-start(f32[136,128]{1,0:T(8,128)S(1)} %get-tuple-element.28), channel_id=1, source_target_pairs={{0,1},{1,0},{2,3},{3,2},{4,5},{5,4},{6,7},{7,6},{8,9},{9,8},{10,11... | collective-permute-start | bytes 208904 | tf_op jit(solution)/shard_map/ppermute | solution.py:21
  57.0 5.4 %collective-permute-start.16 = (f32[136,128]{1,0:T(8,128)S(1)}, f32[136,128]{1,0:T(8,128)S(1)}, u32[]{:S(2)}, u32[]{:S(2)}) collective-permute-start(f32[136,128]{1,0:T(8,128)S(1)} %add.61), channel_id=1, source_target_pairs={{0,6},{1,25},{2,4},{3,27},{4,2},{5,29},{6,0},{7,31},{8,14},{9,17},... | collective-permute-start | bytes 208904 | tf_op jit(solution)/shard_map/ppermute | solution.py:21
  58.0 5.0 %collective-permute-start.15 = (f32[136,128]{1,0:T(8,128)S(1)}, f32[136,128]{1,0:T(8,128)S(1)}, u32[]{:S(2)}, u32[]{:S(2)}) collective-permute-start(f32[136,128]{1,0:T(8,128)S(1)} %add.61), channel_id=1, source_target_pairs={{0,4},{1,17},{2,6},{3,19},{4,0},{5,21},{6,2},{7,23},{8,12},{9,25},... | collective-permute-start | bytes 208904 | tf_op jit(solution)/shard_map/ppermute | solution.py:21
  60.0 4.3 %collective-permute-start.14 = (f32[136,128]{1,0:T(8,128)S(1)}, f32[136,128]{1,0:T(8,128)S(1)}, u32[]{:S(2)}, u32[]{:S(2)}) collective-permute-start(f32[136,128]{1,0:T(8,128)S(1)} %add.61), channel_id=1, source_target_pairs={{0,2},{1,9},{2,0},{3,11},{4,6},{5,13},{6,4},{7,15},{8,10},{9,1},{1... | collective-permute-start | bytes 208904 | tf_op jit(solution)/shard_map/ppermute | solution.py:21
  64.3 6.2 %collective-permute-start.19 = (f32[136,128]{1,0:T(8,128)S(1)}, f32[136,128]{1,0:T(8,128)S(1)}, u32[]{:S(2)}, u32[]{:S(2)}) collective-permute-start(f32[136,128]{1,0:T(8,128)S(1)} %add_add_fusion.1), channel_id=1, source_target_pairs={{0,24},{1,7},{2,26},{3,5},{4,28},{5,3},{6,30},{7,1},{8,16},{9,15},... | collective-permute-start | bytes 208904 | tf_op jit(solution)/shard_map/ppermute | solution.py:21
  67.2 5.2 %collective-permute-start.18 = (f32[136,128]{1,0:T(8,128)S(1)}, f32[136,128]{1,0:T(8,128)S(1)}, u32[]{:S(2)}, u32[]{:S(2)}) collective-permute-start(f32[136,128]{1,0:T(8,128)S(1)} %add_add_fusion.1), channel_id=1, source_target_pairs={{0,16},{1,5},{2,18},{3,7},{4,20},{5,1},{6,22},{7,3},{8,24},{9,13},... | collective-permute-start | bytes 208904 | tf_op jit(solution)/shard_map/ppermute | solution.py:21
  67.2 5.2 %collective-permute-start.17 = (f32[136,128]{1,0:T(8,128)S(1)}, f32[136,128]{1,0:T(8,128)S(1)}, u32[]{:S(2)}, u32[]{:S(2)}) collective-permute-start(f32[136,128]{1,0:T(8,128)S(1)} %add_add_fusion.1), channel_id=1, source_target_pairs={{0,8},{1,3},{2,10},{3,1},{4,12},{5,7},{6,14},{7,5},{8,0},{9,11},{1... | collective-permute-start | bytes 208904 | tf_op jit(solution)/shard_map/ppermute | solution.py:21
  72.4 1.3 %collective-permute-start.20 = (f32[136,128]{1,0:T(8,128)S(1)}, f32[136,128]{1,0:T(8,128)S(1)}, u32[]{:S(2)}, u32[]{:S(2)}) collective-permute-start(f32[136,128]{1,0:T(8,128)S(1)} %add_add_fusion.mine_ref), channel_id=1, source_target_pairs={{0,1},{1,0},{2,3},{3,2},{4,5},{5,4},{6,7},{7,6},{8,9},{9,8},{10,11... | collective-permute-start | bytes 208904 | tf_op jit(solution)/shard_map/ppermute | solution.py:21
where the time goes:
time: 80.8 us; the launch traced here: 80.7 us
  waiting for transfers between devices  43.2 us (53%)
  starting transfers between devices  22.9 us (28%)
  Pallas kernels  13.8 us (17%)
    ppermute x21, waiting for transfers between devices, swap(): lax.ppermute(value, ('rows', 'cols'), [(i, i ^ masks[i % 2]) for i in ran...  43.2 us
    ppermute x21, starting transfers between devices, swap(): lax.ppermute(value, ('rows', 'cols'), [(i, i ^ masks[i % 2]) for i in ran...  22.9 us
    pallas_call x4, Pallas kernels, run(): pl.pallas_call(kernel, out_shape=outs, in_specs=[hbm] * whole + [vmem] *...  13.8 us
  transfers between devices with their start and end apart: 21, of which 12 were waited for; matrix products, arithmetic and copies ran while one was open for 0% of the time, Pallas kernels for 3%

commit v1 on v0

--- a/solution.py
+++ b/solution.py
@@ -130,7 +130,7 @@
     low_refs, basis_refs = refs[:count], refs[count : 2 * count]
     base_ref, high_ref, rest_ref, keep_ref, send_ref, pack_ref = refs[2 * count :]
     snaps, points = base_ref.shape
-    chunk = 256
+    chunk = 512
     for start in range(0, points, chunk):
         cols = slice(start, start + chunk)
         recon = nt_dot(low_refs[0][...], basis_refs[0][cols, :])
@@ -265,11 +265,12 @@
             if skip == LANES:
                 continue
             rows = pl.ds(row_tile * LANES + skip, LANES - skip)
-            used = [(place, value) for place, value in zip(places, right) if place[0] is w_ref or place[1] >= row_tile]
-            wide = tn_dot(left[row_tile - a_tiles[0]], jnp.concatenate([value for _, value in used], axis=1))
-            for index, ((ref, t), _) in enumerate(used):
+            for (ref, t), value in zip(places, right):
+                if ref is a_ref and t < row_tile:
+                    continue
+                update = tn_dot(left[row_tile - a_tiles[0]], value)
                 lanes = pl.ds(t * LANES, LANES)
-                ref[rows, lanes] = ref[rows, lanes] - wide[skip:, index * LANES : (index + 1) * LANES]
+                ref[rows, lanes] = ref[rows, lanes] - update[skip:, :]
 
     def emit(row):
         rows = pl.ds(row * LANES, LANES)

time: 80.8 us -> 80.9 us (level)
  no operation moved by 1% of the time
where the time goes in v1:
time: 80.9 us; the launch traced here: 80.7 us
  waiting for transfers between devices  43.2 us (53%)
  starting transfers between devices  22.9 us (28%)
  Pallas kernels  13.8 us (17%)
    ppermute x21, waiting for transfers between devices, swap(): lax.ppermute(value, ('rows', 'cols'), [(i, i ^ masks[i % 2]) for i in ran...  43.2 us
    ppermute x21, starting transfers between devices, swap(): lax.ppermute(value, ('rows', 'cols'), [(i, i ^ masks[i % 2]) for i in ran...  22.9 us
    pallas_call x4, Pallas kernels, run(): pl.pallas_call(kernel, out_shape=outs, in_specs=[hbm] * whole + [vmem] *...  13.8 us
  transfers between devices with their start and end apart: 21, of which 12 were waited for; matrix products, arithmetic and copies ran while one was open for 0% of the time, Pallas kernels for 3%

profile of v1, /device:TPU:0, one launch (start us, length us, event | category | flops | bytes accessed | tf_op | source)
XLA Modules:
  0.0 80.7 jit_solution(52793951022450732)
XLA Ops:
  0.6 3.0 %shard_map.49 = (f32[64,256]{1,0:T(8,128)S(1)}, f32[64,256]{1,0:T(8,128)S(1)}, f32[64,256]{1,0:T(8,128)S(1)}, f32[64,256]{1,0:T(8,128)S(1)}, bf16[1024,256]{1,0:...) custom-call(bf16[4096,256]{1,0:T(8,128)(2,1)} %basis_ref.3, bf16[256,4096]{1,0:T(8,128)(2,1)} %snaps_ref.3), custom_call_target="tpu_custom_call" | custom-call | flops 536870912 | bytes 6029312 | tf_op jit(solution)/shard_map/pallas_call | solution.py:329
  3.7 3.1 %collective-permute-start = (f32[64,256]{1,0:T(8,128)S(1)}, f32[64,256]{1,0:T(8,128)S(1)}, u32[]{:S(2)}, u32[]{:S(2)}) collective-permute-start(f32[64,256]{1,0:T(8,128)S(1)} %get-tuple-element.19), channel_id=1, source_target_pairs={{0,4},{1,9},{2,6},{3,11},{4,0},{5,13},{6,2},{7,15},{8,12},{9,1},{1... | collective-permute-start | bytes 196616 | tf_op jit(solution)/shard_map/ppermute | solution.py:21
  6.7 1.6 %collective-permute-start.1 = (f32[64,256]{1,0:T(8,128)S(1)}, f32[64,256]{1,0:T(8,128)S(1)}, u32[]{:S(2)}, u32[]{:S(2)}) collective-permute-start(f32[64,256]{1,0:T(8,128)S(1)} %get-tuple-element.20), channel_id=1, source_target_pairs={{0,8},{1,17},{2,10},{3,19},{4,12},{5,21},{6,14},{7,23},{8,0},{9,25... | collective-permute-start | bytes 196616 | tf_op jit(solution)/shard_map/ppermute | solution.py:21
  8.3 0.7 collective-permute-done
  9.0 2.2 %collective-permute-done.1 = f32[64,256]{1,0:T(8,128)S(1)} collective-permute-done((f32[64,256]{1,0:T(8,128)S(1)}, f32[64,256]{1,0:T(8,128)S(1)}, u32[]{:S(2)}, u32[]{:S(2)}) %collective-permute-start.1) | collective-permute-done | bytes 65568 | tf_op jit(solution)/shard_map/ppermute | solution.py:21
  11.2 2.3 %collective-permute-done.2 = f32[64,256]{1,0:T(8,128)S(1)} collective-permute-done((f32[64,256]{1,0:T(8,128)S(1)}, f32[64,256]{1,0:T(8,128)S(1)}, u32[]{:S(2)}, u32[]{:S(2)}) %collective-permute-start.2) | collective-permute-done | bytes 65568 | tf_op jit(solution)/shard_map/ppermute | solution.py:21
  13.5 2.7 %collective-permute-start.3 = (f32[64,256]{1,0:T(8,128)S(1)}, f32[64,256]{1,0:T(8,128)S(1)}, u32[]{:S(2)}, u32[]{:S(2)}) collective-permute-start(f32[64,256]{1,0:T(8,128)S(1)} %add_add_fusion.2), channel_id=1, source_target_pairs={{0,16},{1,5},{2,18},{3,7},{4,20},{5,1},{6,22},{7,3},{8,24},{9,13},... | collective-permute-start | bytes 196616 | tf_op jit(solution)/shard_map/ppermute | solution.py:21
  16.1 3.5 %collective-permute-done.3 = f32[64,256]{1,0:T(8,128)S(1)} collective-permute-done((f32[64,256]{1,0:T(8,128)S(1)}, f32[64,256]{1,0:T(8,128)S(1)}, u32[]{:S(2)}, u32[]{:S(2)}) %collective-permute-start.3) | collective-permute-done | bytes 65568 | tf_op jit(solution)/shard_map/ppermute | solution.py:21
  19.7 0.9 %collective-permute-start.6 = (bf16[64,256]{1,0:T(8,128)(2,1)S(1)}, bf16[64,256]{1,0:T(8,128)(2,1)S(1)}, u32[]{:S(2)}, u32[]{:S(2)}) collective-permute-start(bf16[64,256]{1,0:T(8,128)(2,1)S(1)} %multiply_convert_fusion), channel_id=1, source_target_pairs={{0,12},{1,25},{2,14},{3,27},{4,8},{5,29},{6,10},{7,31},{8,4},{9,17... | collective-permute-start | bytes 98312 | tf_op jit(solution)/shard_map/ppermute | solution.py:21
  20.6 0.2 collective-permute-start.5
  20.8 2.5 %collective-permute-start.4 = (bf16[64,256]{1,0:T(8,128)(2,1)S(1)}, bf16[64,256]{1,0:T(8,128)(2,1)S(1)}, u32[]{:S(2)}, u32[]{:S(2)}) collective-permute-start(bf16[64,256]{1,0:T(8,128)(2,1)S(1)} %multiply_convert_fusion), channel_id=1, source_target_pairs={{0,4},{1,9},{2,6},{3,11},{4,0},{5,13},{6,2},{7,15},{8,12},{9,1},{1... | collective-permute-start | bytes 98312 | tf_op jit(solution)/shard_map/ppermute | solution.py:21
  23.3 1.5 %collective-permute-start.11 = (bf16[1024,256]{1,0:T(8,128)(2,1)S(1)}, bf16[1024,256]{1,0:T(8,128)(2,1)S(1)}, u32[]{:S(2)}, u32[]{:S(2)}) collective-permute-start(bf16[1024,256]{1,0:T(8,128)(2,1)S(1)} %get-tuple-element.24), channel_id=1, source_target_pairs={{0,2},{1,3},{2,0},{3,1},{4,6},{5,7},{6,4},{7,5},{8,10},{9,11},{10,... | collective-permute-start | bytes 1572872 | tf_op jit(solution)/shard_map/ppermute | solution.py:21
  24.8 0.4 collective-permute-start.12
  25.2 1.6 %collective-permute-start.9 = (bf16[256,256]{1,0:T(8,128)(2,1)S(1)}, bf16[256,256]{1,0:T(8,128)(2,1)S(1)}, u32[]{:S(2)}, u32[]{:S(2)}) collective-permute-start(bf16[256,256]{1,0:T(8,128)(2,1)S(1)} %pad_maximum_fusion.low_ref), channel_id=1, source_target_pairs={{0,2},{1,3},{2,0},{3,1},{4,6},{5,7},{6,4},{7,5},{8,10},{9,11},{10,... | collective-permute-start | bytes 393224 | tf_op jit(solution)/shard_map/ppermute | solution.py:21
  26.8 24.9 %collective-permute-done.9.refs_0_ = bf16[256,256]{1,0:T(8,128)(2,1)S(1)} collective-permute-done((bf16[256,256]{1,0:T(8,128)(2,1)S(1)}, bf16[256,256]{1,0:T(8,128)(2,1)S(1)}, u32[]{:S(2)}, u32[]{:S(2)}) %collective-permute-start.9) | collective-permute-done | bytes 131104 | tf_op jit(solution)/shard_map/ppermute | solution.py:21
  51.7 2.3 %shard_map.50 = (f32[256,1024]{1,0:T(8,128)S(1)}, f32[256,256]{1,0:T(8,128)}) custom-call(bf16[4096,256]{1,0:T(8,128)(2,1)} %basis_ref.3, bf16[256,4096]{1,0:T(8,128)(2,1)} %snaps_ref.3, bf16[256,256]{1,0:T(8,128)(2,1)S(1)} %pad_maximum_fusion.low_ref, bf16[256,256]{1,0:T(8,128)(2,1)S(1)} %collective-permute-done.7.near_low_ref, ...), custom_call_target="tpu_custom_call" | custom-call | flops 268435456 | bytes 6291456 | tf_op jit(solution)/shard_map/pallas_call | solution.py:329
  54.0 1.5 %shard_map.51 = (bf16[256,1024]{1,0:T(8,128)(2,1)S(1)}, bf16[256,1024]{1,0:T(8,128)(2,1)S(1)}, f32[136,128]{1,0:T(8,128)S(1)}, f32[136,128]{1,0:T(8,128)S(1)}) custom-call(bf16[256,256]{1,0:T(8,128)(2,1)S(1)} %collective-permute-done.9.refs_0_, bf16[256,256]{1,0:T(8,128)(2,1)S(1)} %collective-permute-done.10.refs_1_, ...), custom_call_target="tpu_custom_call" | custom-call | flops 671088640 | bytes 3547136 | tf_op jit(solution)/shard_map/pallas_call | solution.py:329
  55.5 0.6 collective-permute-start.13
  56.0 0.9 %collective-permute-done.13 = f32[136,128]{1,0:T(8,128)S(1)} collective-permute-done((f32[136,128]{1,0:T(8,128)S(1)}, f32[136,128]{1,0:T(8,128)S(1)}, u32[]{:S(2)}, u32[]{:S(2)}) %collective-permute-start.13) | collective-permute-done | bytes 69664 | tf_op jit(solution)/shard_map/ppermute | solution.py:21
  57.0 1.0 %collective-permute-start.16 = (f32[136,128]{1,0:T(8,128)S(1)}, f32[136,128]{1,0:T(8,128)S(1)}, u32[]{:S(2)}, u32[]{:S(2)}) collective-permute-start(f32[136,128]{1,0:T(8,128)S(1)} %add.61), channel_id=1, source_target_pairs={{0,6},{1,25},{2,4},{3,27},{4,2},{5,29},{6,0},{7,31},{8,14},{9,17},... | collective-permute-start | bytes 208904 | tf_op jit(solution)/shard_map/ppermute | solution.py:21
  58.0 2.0 %collective-permute-start.15 = (f32[136,128]{1,0:T(8,128)S(1)}, f32[136,128]{1,0:T(8,128)S(1)}, u32[]{:S(2)}, u32[]{:S(2)}) collective-permute-start(f32[136,128]{1,0:T(8,128)S(1)} %add.61), channel_id=1, source_target_pairs={{0,4},{1,17},{2,6},{3,19},{4,0},{5,21},{6,2},{7,23},{8,12},{9,25},... | collective-permute-start | bytes 208904 | tf_op jit(solution)/shard_map/ppermute | solution.py:21
  60.0 0.5 collective-permute-start.14
  60.5 1.8 %collective-permute-done.16 = f32[136,128]{1,0:T(8,128)S(1)} collective-permute-done((f32[136,128]{1,0:T(8,128)S(1)}, f32[136,128]{1,0:T(8,128)S(1)}, u32[]{:S(2)}, u32[]{:S(2)}) %collective-permute-start.16) | collective-permute-done | bytes 69664 | tf_op jit(solution)/shard_map/ppermute | solution.py:21
  62.3 0.7 collective-permute-done.15
  63.0 1.3 %collective-permute-done.14 = f32[136,128]{1,0:T(8,128)S(1)} collective-permute-done((f32[136,128]{1,0:T(8,128)S(1)}, f32[136,128]{1,0:T(8,128)S(1)}, u32[]{:S(2)}, u32[]{:S(2)}) %collective-permute-start.14) | collective-permute-done | bytes 69664 | tf_op jit(solution)/shard_map/ppermute | solution.py:21
  64.3 2.9 %collective-permute-start.19 = (f32[136,128]{1,0:T(8,128)S(1)}, f32[136,128]{1,0:T(8,128)S(1)}, u32[]{:S(2)}, u32[]{:S(2)}) collective-permute-start(f32[136,128]{1,0:T(8,128)S(1)} %add_add_fusion.1), channel_id=1, source_target_pairs={{0,24},{1,7},{2,26},{3,5},{4,28},{5,3},{6,30},{7,1},{8,16},{9,15},... | collective-permute-start | bytes 208904 | tf_op jit(solution)/shard_map/ppermute | solution.py:21
  67.2 1.6 %collective-permute-start.17 = (f32[136,128]{1,0:T(8,128)S(1)}, f32[136,128]{1,0:T(8,128)S(1)}, u32[]{:S(2)}, u32[]{:S(2)}) collective-permute-start(f32[136,128]{1,0:T(8,128)S(1)} %add_add_fusion.1), channel_id=1, source_target_pairs={{0,8},{1,3},{2,10},{3,1},{4,12},{5,7},{6,14},{7,5},{8,0},{9,11},{1... | collective-permute-start | bytes 208904 | tf_op jit(solution)/shard_map/ppermute | solution.py:21
  68.8 1.7 %collective-permute-done.19 = f32[136,128]{1,0:T(8,128)S(1)} collective-permute-done((f32[136,128]{1,0:T(8,128)S(1)}, f32[136,128]{1,0:T(8,128)S(1)}, u32[]{:S(2)}, u32[]{:S(2)}) %collective-permute-start.19) | collective-permute-done | bytes 69664 | tf_op jit(solution)/shard_map/ppermute | solution.py:21
  70.5 1.9 %collective-permute-done.18 = f32[136,128]{1,0:T(8,128)S(1)} collective-permute-done((f32[136,128]{1,0:T(8,128)S(1)}, f32[136,128]{1,0:T(8,128)S(1)}, u32[]{:S(2)}, u32[]{:S(2)}) %collective-permute-start.18) | collective-permute-done | bytes 69664 | tf_op jit(solution)/shard_map/ppermute | solution.py:21
  72.4 0.1 collective-permute-start.20
  72.5 1.2 %collective-permute-done.20.other_ref = f32[136,128]{1,0:T(8,128)S(1)} collective-permute-done((f32[136,128]{1,0:T(8,128)S(1)}, f32[136,128]{1,0:T(8,128)S(1)}, u32[]{:S(2)}, u32[]{:S(2)}) %collective-permute-start.20) | collective-permute-done | bytes 69664 | tf_op jit(solution)/shard_map/ppermute | solution.py:21
  73.7 7.0 %shard_map.52 = (f32[256,256]{1,0:T(8,128)}, bf16[256,1024]{1,0:T(8,128)(2,1)}) custom-call(f32[136,128]{1,0:T(8,128)S(1)} %add_add_fusion.mine_ref, f32[136,128]{1,0:T(8,128)S(1)} %collective-permute-done.20.other_ref, bf16[256,1024]{1,0:T(8,128)(2,1)S(1)} %get-tuple-element.29.high_ref, bf16[256,1024]{1,0:T(8,128)(2,1)S(1)} %get-tuple-element.30.rest_ref), custom_call_target="tpu_custom_call" | custom-call | flops 402653184 | bytes 1974272 | tf_op jit(solution)/shard_map/pallas_call | solution.py:329
  (21 shorter events, 0.2 us)
Async XLA Ops:
  3.7 5.3 %collective-permute-start = (f32[64,256]{1,0:T(8,128)S(1)}, f32[64,256]{1,0:T(8,128)S(1)}, u32[]{:S(2)}, u32[]{:S(2)}) collective-permute-start(f32[64,256]{1,0:T(8,128)S(1)} %get-tuple-element.19), channel_id=1, source_target_pairs={{0,4},{1,9},{2,6},{3,11},{4,0},{5,13},{6,2},{7,15},{8,12},{9,1},{1... | collective-permute-start | bytes 196616 | tf_op jit(solution)/shard_map/ppermute | solution.py:21
  6.7 4.4 %collective-permute-start.1 = (f32[64,256]{1,0:T(8,128)S(1)}, f32[64,256]{1,0:T(8,128)S(1)}, u32[]{:S(2)}, u32[]{:S(2)}) collective-permute-start(f32[64,256]{1,0:T(8,128)S(1)} %get-tuple-element.20), channel_id=1, source_target_pairs={{0,8},{1,17},{2,10},{3,19},{4,12},{5,21},{6,14},{7,23},{8,0},{9,25... | collective-permute-start | bytes 196616 | tf_op jit(solution)/shard_map/ppermute | solution.py:21
  8.3 5.2 %collective-permute-start.2 = (f32[64,256]{1,0:T(8,128)S(1)}, f32[64,256]{1,0:T(8,128)S(1)}, u32[]{:S(2)}, u32[]{:S(2)}) collective-permute-start(f32[64,256]{1,0:T(8,128)S(1)} %get-tuple-element.21), channel_id=1, source_target_pairs={{0,12},{1,25},{2,14},{3,27},{4,8},{5,29},{6,10},{7,31},{8,4},{9,17... | collective-permute-start | bytes 196616 | tf_op jit(solution)/shard_map/ppermute | solution.py:21
  13.5 6.2 %collective-permute-start.3 = (f32[64,256]{1,0:T(8,128)S(1)}, f32[64,256]{1,0:T(8,128)S(1)}, u32[]{:S(2)}, u32[]{:S(2)}) collective-permute-start(f32[64,256]{1,0:T(8,128)S(1)} %add_add_fusion.2), channel_id=1, source_target_pairs={{0,16},{1,5},{2,18},{3,7},{4,20},{5,1},{6,22},{7,3},{8,24},{9,13},... | collective-permute-start | bytes 196616 | tf_op jit(solution)/shard_map/ppermute | solution.py:21
  19.7 5.1 %collective-permute-start.6 = (bf16[64,256]{1,0:T(8,128)(2,1)S(1)}, bf16[64,256]{1,0:T(8,128)(2,1)S(1)}, u32[]{:S(2)}, u32[]{:S(2)}) collective-permute-start(bf16[64,256]{1,0:T(8,128)(2,1)S(1)} %multiply_convert_fusion), channel_id=1, source_target_pairs={{0,12},{1,25},{2,14},{3,27},{4,8},{5,29},{6,10},{7,31},{8,4},{9,17... | collective-permute-start | bytes 98312 | tf_op jit(solution)/shard_map/ppermute | solution.py:21
  20.6 4.6 %collective-permute-start.5 = (bf16[64,256]{1,0:T(8,128)(2,1)S(1)}, bf16[64,256]{1,0:T(8,128)(2,1)S(1)}, u32[]{:S(2)}, u32[]{:S(2)}) collective-permute-start(bf16[64,256]{1,0:T(8,128)(2,1)S(1)} %multiply_convert_fusion), channel_id=1, source_target_pairs={{0,8},{1,17},{2,10},{3,19},{4,12},{5,21},{6,14},{7,23},{8,0},{9,25... | collective-permute-start | bytes 98312 | tf_op jit(solution)/shard_map/ppermute | solution.py:21
  20.8 4.4 %collective-permute-start.4 = (bf16[64,256]{1,0:T(8,128)(2,1)S(1)}, bf16[64,256]{1,0:T(8,128)(2,1)S(1)}, u32[]{:S(2)}, u32[]{:S(2)}) collective-permute-start(bf16[64,256]{1,0:T(8,128)(2,1)S(1)} %multiply_convert_fusion), channel_id=1, source_target_pairs={{0,4},{1,9},{2,6},{3,11},{4,0},{5,13},{6,2},{7,15},{8,12},{9,1},{1... | collective-permute-start | bytes 98312 | tf_op jit(solution)/shard_map/ppermute | solution.py:21
  23.3 28.4 %collective-permute-start.8 = (bf16[1024,256]{1,0:T(8,128)(2,1)S(1)}, bf16[1024,256]{1,0:T(8,128)(2,1)S(1)}, u32[]{:S(2)}, u32[]{:S(2)}) collective-permute-start(bf16[1024,256]{1,0:T(8,128)(2,1)S(1)} %get-tuple-element.22), channel_id=1, source_target_pairs={{0,1},{1,0},{2,3},{3,2},{4,5},{5,4},{6,7},{7,6},{8,9},{9,8},{10,11... | collective-permute-start | bytes 1572872 | tf_op jit(solution)/shard_map/ppermute | solution.py:21
  23.3 30.7 %collective-permute-start.11 = (bf16[1024,256]{1,0:T(8,128)(2,1)S(1)}, bf16[1024,256]{1,0:T(8,128)(2,1)S(1)}, u32[]{:S(2)}, u32[]{:S(2)}) collective-permute-start(bf16[1024,256]{1,0:T(8,128)(2,1)S(1)} %get-tuple-element.24), channel_id=1, source_target_pairs={{0,2},{1,3},{2,0},{3,1},{4,6},{5,7},{6,4},{7,5},{8,10},{9,11},{10,... | collective-permute-start | bytes 1572872 | tf_op jit(solution)/shard_map/ppermute | solution.py:21
  24.8 29.2 %collective-permute-start.12 = (bf16[1024,256]{1,0:T(8,128)(2,1)S(1)}, bf16[1024,256]{1,0:T(8,128)(2,1)S(1)}, u32[]{:S(2)}, u32[]{:S(2)}) collective-permute-start(bf16[1024,256]{1,0:T(8,128)(2,1)S(1)} %get-tuple-element.25), channel_id=1, source_target_pairs={{0,3},{1,2},{2,1},{3,0},{4,7},{5,6},{6,5},{7,4},{8,11},{9,10},{10,... | collective-permute-start | bytes 1572872 | tf_op jit(solution)/shard_map/ppermute | solution.py:21
  25.2 26.4 %collective-permute-start.9 = (bf16[256,256]{1,0:T(8,128)(2,1)S(1)}, bf16[256,256]{1,0:T(8,128)(2,1)S(1)}, u32[]{:S(2)}, u32[]{:S(2)}) collective-permute-start(bf16[256,256]{1,0:T(8,128)(2,1)S(1)} %pad_maximum_fusion.low_ref), channel_id=1, source_target_pairs={{0,2},{1,3},{2,0},{3,1},{4,6},{5,7},{6,4},{7,5},{8,10},{9,11},{10,... | collective-permute-start | bytes 393224 | tf_op jit(solution)/shard_map/ppermute | solution.py:21
  26.7 24.9 %collective-permute-start.7 = (bf16[256,256]{1,0:T(8,128)(2,1)S(1)}, bf16[256,256]{1,0:T(8,128)(2,1)S(1)}, u32[]{:S(2)}, u32[]{:S(2)}) collective-permute-start(bf16[256,256]{1,0:T(8,128)(2,1)S(1)} %pad_maximum_fusion.low_ref), channel_id=1, source_target_pairs={{0,1},{1,0},{2,3},{3,2},{4,5},{5,4},{6,7},{7,6},{8,9},{9,8},{10,11... | collective-permute-start | bytes 393224 | tf_op jit(solution)/shard_map/ppermute | solution.py:21
  51.6 2.3 %collective-permute-start.10 = (bf16[256,256]{1,0:T(8,128)(2,1)S(1)}, bf16[256,256]{1,0:T(8,128)(2,1)S(1)}, u32[]{:S(2)}, u32[]{:S(2)}) collective-permute-start(bf16[256,256]{1,0:T(8,128)(2,1)S(1)} %collective-permute-done.9.refs_0_), channel_id=1, source_target_pairs={{0,1},{1,0},{2,3},{3,2},{4,5},{5,4},{6,7},{7,6},{8,9},{9,8},{10,11... | collective-permute-start | bytes 393224 | tf_op jit(solution)/shard_map/ppermute | solution.py:21
  55.5 1.5 %collective-permute-start.13 = (f32[136,128]{1,0:T(8,128)S(1)}, f32[136,128]{1,0:T(8,128)S(1)}, u32[]{:S(2)}, u32[]{:S(2)}) collective-permute-start(f32[136,128]{1,0:T(8,128)S(1)} %get-tuple-element.28), channel_id=1, source_target_pairs={{0,1},{1,0},{2,3},{3,2},{4,5},{5,4},{6,7},{7,6},{8,9},{9,8},{10,11... | collective-permute-start | bytes 208904 | tf_op jit(solution)/shard_map/ppermute | solution.py:21
  57.0 5.4 %collective-permute-start.16 = (f32[136,128]{1,0:T(8,128)S(1)}, f32[136,128]{1,0:T(8,128)S(1)}, u32[]{:S(2)}, u32[]{:S(2)}) collective-permute-start(f32[136,128]{1,0:T(8,128)S(1)} %add.61), channel_id=1, source_target_pairs={{0,6},{1,25},{2,4},{3,27},{4,2},{5,29},{6,0},{7,31},{8,14},{9,17},... | collective-permute-start | bytes 208904 | tf_op jit(solution)/shard_map/ppermute | solution.py:21
  58.0 5.0 %collective-permute-start.15 = (f32[136,128]{1,0:T(8,128)S(1)}, f32[136,128]{1,0:T(8,128)S(1)}, u32[]{:S(2)}, u32[]{:S(2)}) collective-permute-start(f32[136,128]{1,0:T(8,128)S(1)} %add.61), channel_id=1, source_target_pairs={{0,4},{1,17},{2,6},{3,19},{4,0},{5,21},{6,2},{7,23},{8,12},{9,25},... | collective-permute-start | bytes 208904 | tf_op jit(solution)/shard_map/ppermute | solution.py:21
  60.0 4.3 %collective-permute-start.14 = (f32[136,128]{1,0:T(8,128)S(1)}, f32[136,128]{1,0:T(8,128)S(1)}, u32[]{:S(2)}, u32[]{:S(2)}) collective-permute-start(f32[136,128]{1,0:T(8,128)S(1)} %add.61), channel_id=1, source_target_pairs={{0,2},{1,9},{2,0},{3,11},{4,6},{5,13},{6,4},{7,15},{8,10},{9,1},{1... | collective-permute-start | bytes 208904 | tf_op jit(solution)/shard_map/ppermute | solution.py:21
  64.3 6.2 %collective-permute-start.19 = (f32[136,128]{1,0:T(8,128)S(1)}, f32[136,128]{1,0:T(8,128)S(1)}, u32[]{:S(2)}, u32[]{:S(2)}) collective-permute-start(f32[136,128]{1,0:T(8,128)S(1)} %add_add_fusion.1), channel_id=1, source_target_pairs={{0,24},{1,7},{2,26},{3,5},{4,28},{5,3},{6,30},{7,1},{8,16},{9,15},... | collective-permute-start | bytes 208904 | tf_op jit(solution)/shard_map/ppermute | solution.py:21
  67.2 5.2 %collective-permute-start.18 = (f32[136,128]{1,0:T(8,128)S(1)}, f32[136,128]{1,0:T(8,128)S(1)}, u32[]{:S(2)}, u32[]{:S(2)}) collective-permute-start(f32[136,128]{1,0:T(8,128)S(1)} %add_add_fusion.1), channel_id=1, source_target_pairs={{0,16},{1,5},{2,18},{3,7},{4,20},{5,1},{6,22},{7,3},{8,24},{9,13},... | collective-permute-start | bytes 208904 | tf_op jit(solution)/shard_map/ppermute | solution.py:21
  67.2 5.2 %collective-permute-start.17 = (f32[136,128]{1,0:T(8,128)S(1)}, f32[136,128]{1,0:T(8,128)S(1)}, u32[]{:S(2)}, u32[]{:S(2)}) collective-permute-start(f32[136,128]{1,0:T(8,128)S(1)} %add_add_fusion.1), channel_id=1, source_target_pairs={{0,8},{1,3},{2,10},{3,1},{4,12},{5,7},{6,14},{7,5},{8,0},{9,11},{1... | collective-permute-start | bytes 208904 | tf_op jit(solution)/shard_map/ppermute | solution.py:21
  72.4 1.3 %collective-permute-start.20 = (f32[136,128]{1,0:T(8,128)S(1)}, f32[136,128]{1,0:T(8,128)S(1)}, u32[]{:S(2)}, u32[]{:S(2)}) collective-permute-start(f32[136,128]{1,0:T(8,128)S(1)} %add_add_fusion.mine_ref), channel_id=1, source_target_pairs={{0,1},{1,0},{2,3},{3,2},{4,5},{5,4},{6,7},{7,6},{8,9},{9,8},{10,11... | collective-permute-start | bytes 208904 | tf_op jit(solution)/shard_map/ppermute | solution.py:21
